TPU v7x, 32 devices: a whole 2x2x4 slice. The times are simulated.
32 devices in a mesh: dp: 2 (over x), row: 4 (over y, core), col: 4 (over z).
Axes of the slice: x: 2, y: 2, z: 4, core: 2. Of those that a mesh axis runs over, the one named last changes fastest.
Arguments:
- acts: bfloat16 [1024, 8192], P(('dp', 'col'), 'row'), may hold values from -0.5 to 0.5
- grad_out: bfloat16 [1024, 14336], P(('dp', 'row'), 'col'), may hold values from -6 to 6
- weight: bfloat16 [8192, 14336], P('row', 'col'), may hold values from -0.0625 to 0.0625
Outputs:
- grad_input: bfloat16 [1024, 8192], P(('dp', 'col'), 'row')
- grad_weight: bfloat16 [4, 2048, 14336], P('row', 'dp', 'col')
All inputs are finite; a program needn't handle non-finite values.
Results may differ from a plain program's by a relative error of at most 0.001.
Values may be sent and summed in bfloat16 or wider, within the bound.
No kernel may reach another device: no remote copies, remote signals or barrier semaphores. Data moves between devices by JAX's collectives and lax.ppermute only.
A program may use at most 128 MiB of HBM per device.

v0:
```python
import jax
import jax.numpy as jnp
from jax import lax
from jax.sharding import PartitionSpec as P


def shards(acts, grad_out, weight):
    act_local = lax.all_gather(acts, "col", axis=0, tiled=True)
    partial_value = lax.dot_general(
        lax.all_gather(grad_out, "row", axis=0, tiled=True),
        weight,
        (((1,), (1,)), ((), ())),
        preferred_element_type=jnp.float32,
    )
    act_all = lax.all_to_all(act_local, "dp", split_axis=1, concat_axis=0, tiled=True)
    summed = lax.dot_general(
        act_all,
        lax.all_gather(grad_out, ("dp", "row"), axis=0, tiled=True),
        (((0,), (0,)), ((), ())),
        preferred_element_type=jnp.float32,
    )
    grad_weight = summed.astype(jnp.bfloat16)[None]
    grad_input = lax.psum_scatter(partial_value, "col", scatter_dimension=0, tiled=True).astype(
        jnp.bfloat16
    )
    return (grad_input, grad_weight)


def solution(mesh):
    in_specs = (P(("dp", "col"), "row"), P(("dp", "row"), "col"), P("row", "col"))
    out_specs = (P(("dp", "col"), "row"), P("row", "dp", "col"))
    return jax.shard_map(shards, mesh=mesh, in_specs=in_specs, out_specs=out_specs, check_vma=False)
```

profile of v0, /device:TPU:0, one launch (start us, length us, event | category | flops | bytes accessed | tf_op | source)
XLA Modules:
  0.0 239.2 jit_solution(466084870658492629)
XLA Ops:
  7.2 0.0 all-gather.4.cloned.1.call-start
  7.2 0.7 all-gather.4.cloned.1.call-update
  7.9 0.0 all-gather.6.cloned.1.call-start
  7.9 2.0 copy.5
  10.0 0.0 all-gather.6.cloned.1.call-update
  10.0 0.0 all-gather.8.cloned.1.call-start
  10.1 0.7 all-gather.8.cloned.1.call-update
  10.7 0.0 reduce-scatter.2.cloned.1.call-start
  10.8 33.0 %all-gather.4.cloned.1.call-done = bf16[512,3584]{1,0:T(8,128)(2,1)} async-done(((bf16[128,3584]{1,0:T(8,128)(2,1)}), bf16[512,3584]{1,0:T(8,128)(2,1)}) %all-gather.4.cloned.1.call-update) | async-done | bytes 3670032 | tf_op jit(solution)/shard_map/all_gather | solution.py:10
  43.8 13.4 %fusion.1 = f32[512,2048]{1,0:T(8,128)} fusion(bf16[512,3584]{1,0:T(8,128)(2,1)} %all-gather.4.cloned.1.call-done, bf16[2048,3584]{1,0:T(8,128)(2,1)} %param.5), kind=kOutput, calls=%fused_computation.2 | convolution fusion | flops 7516192768 | bytes 22544384 | tf_op jit(solution)/shard_map/dot_general | solution.py:9
  57.2 0.0 reduce-scatter.2.cloned.1.call-update
  57.2 35.0 %all-gather.6.cloned.1.call-done = bf16[512,2048]{0,1:T(8,128)(2,1)} async-done(((bf16[128,2048]{0,1:T(8,128)(2,1)}), bf16[512,2048]{0,1:T(8,128)(2,1)}) %all-gather.6.cloned.1.call-update) | async-done | bytes 2097168 | tf_op jit(solution)/shard_map/all_gather | solution.py:8
  92.2 39.6 %all_to_all.19 = bf16[512,2,1024]{0,2,1:T(8,128)(2,1)S(1)} all-to-all(bf16[512,2,1024]{0,2,1:T(8,128)(2,1)} %bitcast.10), channel_id=1, replica_groups=mesh['dp'=2,'row'=4,'col'=4] {'dp'}, dimensions={1} | all-to-all | bytes 4194304 | tf_op jit(solution)/shard_map/all_to_all | solution.py:15
  131.8 2.5 %copy.6 = bf16[2,512,1024]{2,1,0:T(8,128)(2,1)} copy(bf16[2,512,1024]{1,2,0:T(8,128)(2,1)S(1)} %bitcast.9) | data formatting | bytes 4194304 | tf_op jit(solution)/shard_map/all_to_all | solution.py:15
  134.3 17.7 %all-gather.8.cloned.1.call-done = bf16[1024,3584]{1,0:T(8,128)(2,1)} async-done(((bf16[128,3584]{1,0:T(8,128)(2,1)}), bf16[1024,3584]{1,0:T(8,128)(2,1)}) %all-gather.8.cloned.1.call-update) | async-done | bytes 7340048 | tf_op jit(solution)/shard_map/all_gather | solution.py:18
  151.9 12.6 %fusion = bf16[1,1024,3584]{2,1,0:T(8,128)(2,1)} fusion(bf16[1024,1024]{1,0:T(8,128)(2,1)} %bitcast.11, bf16[1024,3584]{1,0:T(8,128)(2,1)} %all-gather.8.cloned.1.call-done), kind=kOutput, calls=%fused_computation.1 | convolution fusion | flops 7519862784 | bytes 16777216 | tf_op jit(solution)/shard_map/dot_general | solution.py:16
  164.6 66.0 %reduce-scatter.2.cloned.1.call-done = f32[128,2048]{1,0:T(8,128)} async-done(((f32[512,2048]{1,0:T(8,128)}), f32[128,2048]{1,0:T(8,128)}) %reduce-scatter.2.cloned.1.call-update) | async-done | bytes 1048592 | tf_op jit(solution)/shard_map/reduce_scatter | solution.py:23
  230.6 2.1 convert_element_type.6
Async XLA Ops:
  7.2 36.6 %all-gather.4.cloned.1.call-start = ((), (), s32[]{:S(2)}) async-start(), calls=%async_computation.2 | async-start | bytes 4587520 | tf_op jit(solution)/shard_map/all_gather | solution.py:10
  7.9 84.3 %all-gather.6.cloned.1.call-start = ((), (), s32[]{:S(2)}) async-start(), calls=%async_computation.4 | async-start | bytes 2621440 | tf_op jit(solution)/shard_map/all_gather | solution.py:8
  10.0 141.9 %all-gather.8.cloned.1.call-start = ((), (), s32[]{:S(2)}) async-start(), calls=%async_computation.5 | async-start | bytes 8257536 | tf_op jit(solution)/shard_map/all_gather | solution.py:18
  10.7 219.8 %reduce-scatter.2.cloned.1.call-start = ((), (), s32[]{:S(2)}) async-start(), calls=%async_computation.3 | async-start | bytes 5242880 | tf_op jit(solution)/shard_map/reduce_scatter | solution.py:23
Sparse Core Ops, SparseCore 0:
  9.5 34.1 all-gather.3
  45.9 46.2 all-gather.5
  94.1 57.7 all-gather.7
  154.1 76.4 reduce-scatter.1
where the time goes:
time: 239 us
  waiting for transfers between devices  153 us (64%)
  blocking collectives  39.6 us (17%)
  matrix products  26 us (11%)
  between operations  13.8 us (6%)
  local copies, waits for them, and re-layouts  4.51 us (2%)
    reduce_scatter x1, waiting for transfers between devices, shards(): lax.psum_scatter(partial_value, 'col', scatter_dimension=0, tiled=True)  66 us
    all_to_all x1, blocking collectives, shards(): lax.all_to_all(act_local, 'dp', split_axis=1, concat_axis=0, tiled=True)  39.6 us
    all_gather x1, waiting for transfers between devices, shards(): act_local = lax.all_gather(acts, 'col', axis=0, tiled=True)  35 us
    all_gather x1, waiting for transfers between devices, shards(): lax.all_gather(grad_out, 'row', axis=0, tiled=True)  33 us
    all_gather x1, waiting for transfers between devices, shards(): lax.all_gather(grad_out, ('dp', 'row'), axis=0, tiled=True)  17.7 us
    dot_general x1, matrix products, shards(): lax.dot_general(lax.all_gather(grad_out, 'row', axis=0, tiled=True), weig...  13.4 us
    dot_general x1, matrix products, shards(): lax.dot_general(act_all, lax.all_gather(grad_out, ('dp', 'row'), axis=0,...  12.6 us
  transfers between devices with their start and end apart: 4, of which 4 were waited for; matrix products, arithmetic and copies ran while one was open for 13% of the time, Pallas kernels for 0%

commit v1 on v0

--- a/solution.py
+++ b/solution.py
@@ -2,9 +2,42 @@
 import jax.numpy as jnp
 from jax import lax
 from jax.sharding import PartitionSpec as P
+from jax.lax import axis_index, axis_size, ppermute
+
+
+def form_runs(chunk, dim_i):
+    chunk = jnp.moveaxis(chunk, 0, dim_i)
+    block_next = chunk.shape
+    block_now = chunk.reshape(
+        *block_next[:dim_i], block_next[dim_i] * block_next[dim_i + 1], *block_next[dim_i + 2 :]
+    )
+    return block_now
 
 
 def shards(acts, grad_out, weight):
+
+    def enter_pieces_all(original, axis_tag, dim_k):
+        devs = axis_size(axis_tag)
+        block_last = range(devs)
+        right_arr = map(lambda d: (d, (d + 1) % devs), block_last)
+        pool = list(right_arr)
+        gallery = [(i0, hop_no) for hop_no, i0 in pool]
+        oldest, mid_arr = ([], [])
+        for p in [*range(devs - 1)]:
+            if p % 2 == 0:
+                reply = ppermute(oldest[-1] if oldest else original, axis_tag, pool)
+                oldest.append(reply)
+            else:
+                work_now = ppermute(mid_arr[-1] if mid_arr else original, axis_tag, gallery)
+                mid_arr.append(work_now)
+        k_now = jnp.stack([*oldest[::-1], original, *mid_arr])
+        x_now = axis_index(axis_tag)
+        upper = len(oldest)
+        item_now = x_now - upper
+        k_now = k_now[(jnp.arange(devs) - item_now) % devs]
+        w2 = form_runs(k_now, dim_k)
+        return w2
+
     act_local = lax.all_gather(acts, "col", axis=0, tiled=True)
     partial_value = lax.dot_general(
         lax.all_gather(grad_out, "row", axis=0, tiled=True),
@@ -15,7 +48,7 @@
     act_all = lax.all_to_all(act_local, "dp", split_axis=1, concat_axis=0, tiled=True)
     summed = lax.dot_general(
         act_all,
-        lax.all_gather(grad_out, ("dp", "row"), axis=0, tiled=True),
+        enter_pieces_all(grad_out, ("dp", "row"), 0),
         (((0,), (0,)), ((), ())),
         preferred_element_type=jnp.float32,
     )

time: 239 us -> 212 us (0.89)
  waiting for transfers between devices: 153 us -> 86.6 us
  starting transfers between devices: 0.16 us -> 44.5 us
  blocking collectives: 39.6 us -> 0 us
  local copies, waits for them, and re-layouts: 4.51 us -> 37.9 us
    ppermute x0 -> x7, starting transfers between devices: none -> 40.6 us  [the longest x4 37.9 us: enter_pieces_all(): reply = ppermute(oldest[-1] if oldest else original, axis_tag, pool)]
    all_to_all x1 -> x0, blocking collectives: 39.6 us -> none  [shards(): lax.all_to_all(act_local, 'dp', split_axis=1, concat_axis=0, tiled=True)]
    all_gather x1, waiting for transfers between devices: 35 us -> 0.02 us  [shards(): act_local = lax.all_gather(acts, 'col', axis=0, tiled=True)]
    ppermute x0 -> x7, waiting for transfers between devices: none -> 31.3 us  [the longest x4 31.2 us: enter_pieces_all(): reply = ppermute(oldest[-1] if oldest else original, axis_tag, pool)]
    reduce_scatter x1, waiting for transfers between devices: 66 us -> 38.6 us  [shards(): lax.psum_scatter(partial_value, 'col', scatter_dimension=0, tiled=True)]
    unnamed x1 -> x21, local copies, waits for them, and re-layouts: 2.04 us -> 25.9 us
    all_gather x1 -> x0, waiting for transfers between devices: 17.7 us -> none  [shards(): lax.all_gather(grad_out, ('dp', 'row'), axis=0, tiled=True)]
    all_gather x1, waiting for transfers between devices: 33 us -> 15.9 us  [shards(): lax.all_gather(grad_out, 'row', axis=0, tiled=True)]
  transfers between devices with their start and end apart: 4 -> 11, of which waited for: 4 -> 5; matrix products, arithmetic and copies ran while one was open for 13% -> 29% of each run, Pallas kernels for 0% -> 0%
where the time goes in v1:
time: 212 us; the launch traced here: 211 us
  waiting for transfers between devices  86.6 us (41%)
  starting transfers between devices  44.5 us (21%)
  local copies, waits for them, and re-layouts  37.9 us (18%)
  matrix products  26 us (12%)
  between operations  13.8 us (7%)
    reduce_scatter x1, waiting for transfers between devices, shards(): lax.psum_scatter(partial_value, 'col', scatter_dimension=0, tiled=True)  38.6 us
    ppermute x4, starting transfers between devices, enter_pieces_all(): reply = ppermute(oldest[-1] if oldest else original, axis_tag, pool)  37.9 us
    ppermute x4, waiting for transfers between devices, enter_pieces_all(): reply = ppermute(oldest[-1] if oldest else original, axis_tag, pool)  31.2 us
    unnamed x21, local copies, waits for them, and re-layouts  25.9 us
    all_gather x1, waiting for transfers between devices, shards(): lax.all_gather(grad_out, 'row', axis=0, tiled=True)  15.9 us
    dot_general x1, matrix products, shards(): lax.dot_general(lax.all_gather(grad_out, 'row', axis=0, tiled=True), weig...  13.4 us
    dot_general x1, matrix products, shards(): lax.dot_general(act_all, enter_pieces_all(grad_out, ('dp', 'row'), 0), ((...  12.7 us
    gather x1, local copies, waits for them, and re-layouts, enter_pieces_all(): k_now = k_now[(jnp.arange(devs) - item_now) % devs]  7.45 us
  transfers between devices with their start and end apart: 11, of which 5 were waited for; matrix products, arithmetic and copies ran while one was open for 29% of the time, Pallas kernels for 0%

profile of v1, /device:TPU:0, one launch (start us, length us, event | category | flops | bytes accessed | tf_op | source)
XLA Modules:
  0.0 210.9 jit_solution(14790507804208361491)
XLA Ops:
  7.2 0.0 all-gather.5.cloned.1.call-start
  7.2 2.0 copy.7
  9.3 0.0 all-gather.3.cloned.1.call-start
  9.3 0.7 all-gather.3.cloned.1.call-update
  10.0 0.5 collective-permute-start
  10.6 14.2 %collective-permute-done = bf16[128,3584]{1,0:T(8,128)(2,1)S(1)} collective-permute-done((bf16[128,3584]{1,0:T(8,128)(2,1)}, bf16[128,3584]{1,0:T(8,128)(2,1)S(1)}, u32[]{:S(2)}, u32[]{:S(2)}) %collective-permute-start) | collective-permute-done | bytes 917536 | tf_op jit(solution)/shard_map/ppermute | solution.py:28
  24.7 0.9 copy-done.1
  25.7 2.6 %collective-permute-start.4 = (bf16[128,3584]{1,0:T(8,128)(2,1)}, bf16[128,3584]{1,0:T(8,128)(2,1)S(1)}, u32[]{:S(2)}, u32[]{:S(2)}) collective-permute-start(bf16[128,3584]{1,0:T(8,128)(2,1)} %param.4), channel_id=1, source_target_pairs={{4,0},{8,4},{12,8},{16,12},{20,16},{24,20},{28,24},{0,28},{5,1},{9... | collective-permute-start | bytes 2752520 | tf_op jit(solution)/shard_map/ppermute | solution.py:31
  28.3 11.2 %collective-permute-done.1 = bf16[128,3584]{1,0:T(8,128)(2,1)S(1)} collective-permute-done((bf16[128,3584]{1,0:T(8,128)(2,1)S(1)}, bf16[128,3584]{1,0:T(8,128)(2,1)S(1)}, u32[]{:S(2)}, u32[]{:S(2)}) %collective-permute-start.1) | collective-permute-done | bytes 917536 | tf_op jit(solution)/shard_map/ppermute | solution.py:28
  39.5 7.8 %collective-permute-start.2 = (bf16[128,3584]{1,0:T(8,128)(2,1)S(1)}, bf16[128,3584]{1,0:T(8,128)(2,1)S(1)}, u32[]{:S(2)}, u32[]{:S(2)}) collective-permute-start(bf16[128,3584]{1,0:T(8,128)(2,1)S(1)} %collective-permute-done.1), channel_id=1, source_target_pairs={{0,4},{4,8},{8,12},{12,16},{16,20},{20,24},{24,28},{28,0},{1,5},{5... | collective-permute-start | bytes 2752520 | tf_op jit(solution)/shard_map/ppermute | solution.py:28
  47.3 0.1 collective-permute-start.5
  47.4 5.9 %collective-permute-done.2 = bf16[128,3584]{1,0:T(8,128)(2,1)S(1)} collective-permute-done((bf16[128,3584]{1,0:T(8,128)(2,1)S(1)}, bf16[128,3584]{1,0:T(8,128)(2,1)S(1)}, u32[]{:S(2)}, u32[]{:S(2)}) %collective-permute-start.2) | collective-permute-done | bytes 917536 | tf_op jit(solution)/shard_map/ppermute | solution.py:28
  53.3 29.5 %collective-permute-start.3 = (bf16[128,3584]{1,0:T(8,128)(2,1)S(1)}, bf16[128,3584]{1,0:T(8,128)(2,1)}, u32[]{:S(2)}, u32[]{:S(2)}) collective-permute-start(bf16[128,3584]{1,0:T(8,128)(2,1)S(1)} %collective-permute-done.2), channel_id=1, source_target_pairs={{0,4},{4,8},{8,12},{12,16},{16,20},{20,24},{24,28},{28,0},{1,5},{5... | collective-permute-start | bytes 2752520 | tf_op jit(solution)/shard_map/ppermute | solution.py:28
  82.8 0.1 collective-permute-start.6
  82.9 3.8 %all-to-all-start = ((bf16[512,2,1024]{0,2,1:T(8,128)(2,1)}), bf16[512,2,1024]{0,2,1:T(8,128)(2,1)S(1)}, u32[]{:S(2)}, u32[]{:S(2)}) async-start(bf16[512,2,1024]{0,2,1:T(8,128)(2,1)} %bitcast.32), calls=%async_computation.1 | async-start | bytes 4194304 | tf_op jit(solution)/shard_map/all_to_all | solution.py:48
  86.7 0.0 reduce-scatter.2.cloned.1.call-start
  86.8 2.2 %bitcast_dynamic-update-slice_fusion.7 = bf16[8,128,3584]{2,1,0:T(8,128)(2,1)} fusion(bf16[128,3584]{1,0:T(8,128)(2,1)} %collective-permute-done.3), kind=kLoop, calls=%fused_computation.10 | loop fusion | bytes 1835008
  89.0 15.9 %all-gather.3.cloned.1.call-done = bf16[512,3584]{1,0:T(8,128)(2,1)} async-done(((bf16[128,3584]{1,0:T(8,128)(2,1)}), bf16[512,3584]{1,0:T(8,128)(2,1)}) %all-gather.3.cloned.1.call-update) | async-done | bytes 3670032 | tf_op jit(solution)/shard_map/all_gather | solution.py:43
  104.9 13.4 %fusion.3 = f32[512,2048]{1,0:T(8,128)} fusion(bf16[512,3584]{1,0:T(8,128)(2,1)} %all-gather.3.cloned.1.call-done, bf16[2048,3584]{1,0:T(8,128)(2,1)} %param.5), kind=kOutput, calls=%fused_computation.18 | convolution fusion | flops 7516192768 | bytes 22544384 | tf_op jit(solution)/shard_map/dot_general | solution.py:42
  118.3 2.3 %bitcast_dynamic-update-slice_fusion.6 = bf16[8,128,3584]{2,1,0:T(8,128)(2,1)} fusion(bf16[8,128,3584]{2,1,0:T(8,128)(2,1)} %bitcast_dynamic-update-slice_fusion.7, bf16[128,3584]{1,0:T(8,128)(2,1)} %copy-done.5), kind=kLoop, calls=%fused_computation.9 | loop fusion | bytes 1835008
  120.6 2.2 %bitcast_dynamic-update-slice_fusion.5 = bf16[8,128,3584]{2,1,0:T(8,128)(2,1)} fusion(bf16[8,128,3584]{2,1,0:T(8,128)(2,1)} %bitcast_dynamic-update-slice_fusion.6, bf16[128,3584]{1,0:T(8,128)(2,1)} %copy-done.4), kind=kLoop, calls=%fused_computation.8 | loop fusion | bytes 1835008
  122.8 2.2 %bitcast_dynamic-update-slice_fusion.4 = bf16[8,128,3584]{2,1,0:T(8,128)(2,1)} fusion(bf16[8,128,3584]{2,1,0:T(8,128)(2,1)} %bitcast_dynamic-update-slice_fusion.5, bf16[128,3584]{1,0:T(8,128)(2,1)} %copy-done.1), kind=kLoop, calls=%fused_computation.7 | loop fusion | bytes 1835008
  124.9 1.0 bitcast_dynamic-update-slice_fusion.3
  125.9 1.0 bitcast_dynamic-update-slice_fusion.2
  126.9 2.2 %bitcast_dynamic-update-slice_fusion.1 = bf16[8,128,3584]{2,1,0:T(8,128)(2,1)} fusion(bf16[8,128,3584]{2,1,0:T(8,128)(2,1)} %bitcast_dynamic-update-slice_fusion.2, bf16[128,3584]{1,0:T(8,128)(2,1)} %collective-permute-done.5), kind=kLoop, calls=%fused_computation.4 | loop fusion | bytes 1835008
  129.1 2.2 %bitcast_dynamic-update-slice_fusion = bf16[8,128,3584]{2,1,0:T(8,128)(2,1)} fusion(bf16[8,128,3584]{2,1,0:T(8,128)(2,1)} %bitcast_dynamic-update-slice_fusion.1, bf16[128,3584]{1,0:T(8,128)(2,1)} %collective-permute-done.6), kind=kLoop, calls=%fused_computation.3 | loop fusion | bytes 1835008 | tf_op jit(solution)/shard_map/stack | solution.py:33
  131.2 7.5 %gather_fusion = bf16[8,128,3584]{2,1,0:T(8,128)(2,1)} fusion(bf16[8,128,3584]{2,1,0:T(8,128)(2,1)} %bitcast_dynamic-update-slice_fusion, s32[1024]{0:T(1024)S(1)} %pad_clamp_fusion), kind=kCustom, calls=%fused_computation | custom fusion | bytes 14680096 | tf_op jit(solution)/shard_map/gather | solution.py:37
  138.7 2.4 %copy.8 = bf16[2,512,1024]{2,1,0:T(8,128)(2,1)} copy(bf16[2,512,1024]{1,2,0:T(8,128)(2,1)S(1)} %bitcast.30) | data formatting | bytes 4194304 | tf_op jit(solution)/shard_map/all_to_all | solution.py:48
  141.0 12.7 %fusion = bf16[1,1024,3584]{1,2,0:T(8,128)(2,1)} fusion(bf16[1024,3584]{1,0:T(8,128)(2,1)} %bitcast.31, bf16[1024,1024]{1,0:T(8,128)(2,1)} %bitcast.33), kind=kOutput, calls=%fused_computation.2 | convolution fusion | flops 7519862784 | bytes 16777216 | tf_op jit(solution)/shard_map/dot_general | solution.py:49
  153.7 10.0 %copy.9 = bf16[1,1024,3584]{2,1,0:T(8,128)(2,1)} copy(bf16[1,1024,3584]{1,2,0:T(8,128)(2,1)} %fusion) | data formatting | bytes 14680064
  163.7 38.6 %reduce-scatter.2.cloned.1.call-done = f32[128,2048]{1,0:T(8,128)} async-done(((f32[512,2048]{1,0:T(8,128)}), f32[128,2048]{1,0:T(8,128)}) %reduce-scatter.2.cloned.1.call-update) | async-done | bytes 1048592 | tf_op jit(solution)/shard_map/reduce_scatter | solution.py:56
  202.3 2.1 convert_element_type.9
  (22 shorter events, 0.1 us)
Async XLA Ops:
  7.2 75.8 %all-gather.5.cloned.1.call-start = ((), (), s32[]{:S(2)}) async-start(), calls=%async_computation.4 | async-start | bytes 2621440 | tf_op jit(solution)/shard_map/all_gather | solution.py:41
  9.3 95.6 %all-gather.3.cloned.1.call-start = ((), (), s32[]{:S(2)}) async-start(), calls=%async_computation.2 | async-start | bytes 4587520 | tf_op jit(solution)/shard_map/all_gather | solution.py:43
  10.0 14.7 %collective-permute-start = (bf16[128,3584]{1,0:T(8,128)(2,1)}, bf16[128,3584]{1,0:T(8,128)(2,1)S(1)}, u32[]{:S(2)}, u32[]{:S(2)}) collective-permute-start(bf16[128,3584]{1,0:T(8,128)(2,1)} %param.4), channel_id=1, source_target_pairs={{0,4},{4,8},{8,12},{12,16},{16,20},{20,24},{24,28},{28,0},{1,5},{5... | collective-permute-start | bytes 2752520 | tf_op jit(solution)/shard_map/ppermute | solution.py:28
  24.7 0.9 copy-start.1
  25.7 13.8 %collective-permute-start.1 = (bf16[128,3584]{1,0:T(8,128)(2,1)S(1)}, bf16[128,3584]{1,0:T(8,128)(2,1)S(1)}, u32[]{:S(2)}, u32[]{:S(2)}) collective-permute-start(bf16[128,3584]{1,0:T(8,128)(2,1)S(1)} %collective-permute-done), channel_id=1, source_target_pairs={{0,4},{4,8},{8,12},{12,16},{16,20},{20,24},{24,28},{28,0},{1,5},{5... | collective-permute-start | bytes 2752520 | tf_op jit(solution)/shard_map/ppermute | solution.py:28
  25.7 21.7 %collective-permute-start.4 = (bf16[128,3584]{1,0:T(8,128)(2,1)}, bf16[128,3584]{1,0:T(8,128)(2,1)S(1)}, u32[]{:S(2)}, u32[]{:S(2)}) collective-permute-start(bf16[128,3584]{1,0:T(8,128)(2,1)} %param.4), channel_id=1, source_target_pairs={{4,0},{8,4},{12,8},{16,12},{20,16},{24,20},{28,24},{0,28},{5,1},{9... | collective-permute-start | bytes 2752520 | tf_op jit(solution)/shard_map/ppermute | solution.py:31
  39.5 7.8 %copy-start.4 = (bf16[128,3584]{1,0:T(8,128)(2,1)}, bf16[128,3584]{1,0:T(8,128)(2,1)S(1)}, u32[]{:S(2)}) copy-start(bf16[128,3584]{1,0:T(8,128)(2,1)S(1)} %collective-permute-done.1) | copy-start | bytes 2752516
  39.5 13.8 %collective-permute-start.2 = (bf16[128,3584]{1,0:T(8,128)(2,1)S(1)}, bf16[128,3584]{1,0:T(8,128)(2,1)S(1)}, u32[]{:S(2)}, u32[]{:S(2)}) collective-permute-start(bf16[128,3584]{1,0:T(8,128)(2,1)S(1)} %collective-permute-done.1), channel_id=1, source_target_pairs={{0,4},{4,8},{8,12},{12,16},{16,20},{20,24},{24,28},{28,0},{1,5},{5... | collective-permute-start | bytes 2752520 | tf_op jit(solution)/shard_map/ppermute | solution.py:28
  47.3 35.6 %copy-start.2 = (bf16[128,3584]{1,0:T(8,128)(2,1)}, bf16[128,3584]{1,0:T(8,128)(2,1)S(1)}, u32[]{:S(2)}) copy-start(bf16[128,3584]{1,0:T(8,128)(2,1)S(1)} %collective-permute-done.4) | copy-start | bytes 2752516
  47.3 35.5 %collective-permute-start.5 = (bf16[128,3584]{1,0:T(8,128)(2,1)S(1)}, bf16[128,3584]{1,0:T(8,128)(2,1)}, u32[]{:S(2)}, u32[]{:S(2)}) collective-permute-start(bf16[128,3584]{1,0:T(8,128)(2,1)S(1)} %collective-permute-done.4), channel_id=1, source_target_pairs={{4,0},{8,4},{12,8},{16,12},{20,16},{24,20},{28,24},{0,28},{5,1},{9... | collective-permute-start | bytes 2752520 | tf_op jit(solution)/shard_map/ppermute | solution.py:31
  53.3 51.6 %copy-start.5 = (bf16[128,3584]{1,0:T(8,128)(2,1)}, bf16[128,3584]{1,0:T(8,128)(2,1)S(1)}, u32[]{:S(2)}) copy-start(bf16[128,3584]{1,0:T(8,128)(2,1)S(1)} %collective-permute-done.2) | copy-start | bytes 2752516
  53.3 33.5 %collective-permute-start.3 = (bf16[128,3584]{1,0:T(8,128)(2,1)S(1)}, bf16[128,3584]{1,0:T(8,128)(2,1)}, u32[]{:S(2)}, u32[]{:S(2)}) collective-permute-start(bf16[128,3584]{1,0:T(8,128)(2,1)S(1)} %collective-permute-done.2), channel_id=1, source_target_pairs={{0,4},{4,8},{8,12},{12,16},{16,20},{20,24},{24,28},{28,0},{1,5},{5... | collective-permute-start | bytes 2752520 | tf_op jit(solution)/shard_map/ppermute | solution.py:28
  82.8 46.2 %collective-permute-start.6 = (bf16[128,3584]{1,0:T(8,128)(2,1)}, bf16[128,3584]{1,0:T(8,128)(2,1)}, u32[]{:S(2)}, u32[]{:S(2)}) collective-permute-start(bf16[128,3584]{1,0:T(8,128)(2,1)} %collective-permute-done.5), channel_id=1, source_target_pairs={{4,0},{8,4},{12,8},{16,12},{20,16},{24,20},{28,24},{0,28},{5,1},{9... | collective-permute-start | bytes 2752520 | tf_op jit(solution)/shard_map/ppermute | solution.py:31
  82.9 55.7 %all-to-all-start = ((bf16[512,2,1024]{0,2,1:T(8,128)(2,1)}), bf16[512,2,1024]{0,2,1:T(8,128)(2,1)S(1)}, u32[]{:S(2)}, u32[]{:S(2)}) async-start(bf16[512,2,1024]{0,2,1:T(8,128)(2,1)} %bitcast.32), calls=%async_computation.1 | async-start | bytes 4194304 | tf_op jit(solution)/shard_map/all_to_all | solution.py:48
  86.7 115.6 %reduce-scatter.2.cloned.1.call-start = ((), (), s32[]{:S(2)}) async-start(), calls=%async_computation.3 | async-start | bytes 5242880 | tf_op jit(solution)/shard_map/reduce_scatter | solution.py:56
  118.3 6.7 %copy-start = (bf16[128,3584]{1,0:T(8,128)(2,1)S(1)}, bf16[128,3584]{1,0:T(8,128)(2,1)}, u32[]{:S(2)}) copy-start(bf16[128,3584]{1,0:T(8,128)(2,1)} %param.4) | copy-start | bytes 2752516
  118.3 7.6 %copy-start.3 = (bf16[128,3584]{1,0:T(8,128)(2,1)S(1)}, bf16[128,3584]{1,0:T(8,128)(2,1)}, u32[]{:S(2)}) copy-start(bf16[128,3584]{1,0:T(8,128)(2,1)} %copy-done.2) | copy-start | bytes 2752516
Sparse Core Ops, SparseCore 0:
  10.1 48.9 all-gather.4
  60.7 44.1 all-gather.2
  118.4 83.8 reduce-scatter.1
